TPU v7x, 32 devices: a whole 2x2x4 slice. The times are simulated.
32 devices in a mesh: req: 4 (over z), seq: 8 (over y, x, core).
Axes of the slice: x: 2, y: 2, z: 4, core: 2. Of those that a mesh axis runs over, the one named last changes fastest.
Arguments:
- hidden_in: bfloat16 [4, 32, 4, 2048], P(None, 'req', None, 'seq'), may hold values from -30 to 30
- cache_lens: int32 [32], P('req'), may hold values from 1 to 4092, as said below
- page_table: int32 [32, 32], P('req'), may hold values from -1 to 55, as said below
- key_cache: bfloat16 [224, 128, 1024], P(('req', 'seq')), may hold values from -250 to 250
- value_cache: bfloat16 [224, 128, 1024], P(('req', 'seq')), may hold values from -4 to 4
- norm_attn: float32 [8192], replicated, may hold values from 0.1 to 1.9
- w_qkv: bfloat16 [8192, 10240], P(None, 'seq'), may hold values from -0.0625 to 0.0625
- b_qkv: bfloat16 [10240], P('seq'), may hold values from -3 to 3
- w_out: bfloat16 [8192, 4, 2048], P(None, None, 'seq'), may hold values from -0.25 to 0.25
- norm_mlp: float32 [8192], replicated, may hold values from 0.1 to 1.9
- w_gate: bfloat16 [8192, 29568], P('req', 'seq'), may hold values from -0.0625 to 0.0625
- w_up: bfloat16 [8192, 29568], P('req', 'seq'), may hold values from -0.0625 to 0.0625
- w_down: bfloat16 [29568, 8192], P('seq', 'req'), may hold values from -0.03125 to 0.03125
Outputs:
- hidden_out: bfloat16 [4, 32, 4, 2048], P(None, 'req', None, 'seq')
- key_cache_out: bfloat16 [224, 128, 1024], P(('req', 'seq'))
- value_cache_out: bfloat16 [224, 128, 1024], P(('req', 'seq'))
Inputs may be any that keep to these rules, and one draw needn't show every extreme that they name: `cache_lens`: in each group of 8 requests exactly one holds 4092 tokens and one holds 380; every other one holds at most 380. For request r and logical page j below ceil((cache_lens[r]+4)/128), page_table[r, j] is a slot of the group's 56 page slots (slot s*7+p is the p-th slot of seq index s); no slot is named twice within a group; all other entries are -1.
All inputs are finite; a program needn't handle non-finite values.
Results may differ from a plain program's by a relative error of at most 0.012.
The roundings to bfloat16 on the way count: a program that leaves them out, or rounds other values in their place, can miss the bound.
Values may be sent and summed in bfloat16 or wider, within the bound.
A program may use at most 320 MiB of HBM per device.

v0:
```python
import math
import jax
import jax.numpy as jnp
from jax import lax
from jax.sharding import PartitionSpec as P

D = 8192
H = 64
KV = 8
HD = 128
STEPS = 4
EPSILON = 1e-06
THETA = 1000000.0
NEGATIVE = -1e30


def rotate(heads, position):
    half = heads.shape[-1] // 2
    freq = THETA ** (-(jnp.arange(half, dtype=jnp.float32) * 2.0 / heads.shape[-1]))
    angle = position.astype(jnp.float32)[:, None, None] * freq[None, None, :]
    cosine = jnp.cos(angle)
    sine = jnp.sin(angle)
    first = heads[..., :half]
    second = heads[..., half:]
    return jnp.concatenate(
        [first * cosine - second * sine, second * cosine + first * sine], axis=-1
    )


def on_device(
    hidden_in,
    cache_lens,
    page_table,
    key_cache,
    value_cache,
    norm_attn,
    w_qkv,
    b_qkv,
    w_out,
    norm_mlp,
    w_gate,
    w_up,
    w_down,
):
    steps, requests, blocks, pieces = hidden_in.shape
    rows = steps * requests
    slots, per_page, _ = key_cache.shape
    group = H // KV
    quarter = D // blocks
    seq = quarter // pieces
    scale = 1.0 / math.sqrt(HD)
    slot_ids = lax.axis_index("seq") * slots + jnp.arange(slots, dtype=jnp.int32)
    matches = page_table[:, :, None] == slot_ids[None, None, :]
    live = jnp.any(matches, axis=(0, 1))
    owner = jnp.sum(
        jnp.where(matches, jnp.arange(requests, dtype=jnp.int32)[:, None, None], 0), axis=(0, 1)
    )
    logical = jnp.sum(
        jnp.where(matches, jnp.arange(page_table.shape[1], dtype=jnp.int32)[None, :, None], 0),
        axis=(0, 1),
    )
    owned = jnp.logical_and(
        jnp.arange(requests, dtype=jnp.int32)[None, :] == owner[:, None], live[:, None]
    )
    slot_length = jnp.sum(jnp.where(owned, cache_lens[None, :], 0), axis=1)
    positions = logical[:, None] * per_page + jnp.arange(per_page, dtype=jnp.int32)[None, :]
    flat = lax.all_gather(hidden_in, "seq", axis=3, tiled=True).reshape(rows, D).astype(jnp.float32)
    normed = (
        flat * lax.rsqrt(jnp.mean(flat * flat, axis=1, keepdims=True) + EPSILON) * norm_attn
    ).astype(jnp.bfloat16)
    columns = (
        jnp.dot(normed, w_qkv, preferred_element_type=jnp.float32) + b_qkv.astype(jnp.float32)
    ).astype(jnp.bfloat16)
    projected = lax.all_gather(columns, "seq", axis=1, tiled=True)
    position = (jnp.arange(steps, dtype=jnp.int32)[:, None] + cache_lens[None, :]).reshape(rows)
    rotated = rotate(
        projected[:, : (H + KV) * HD].reshape(rows, H + KV, HD).astype(jnp.float32), position
    ).astype(jnp.bfloat16)
    queries = rotated[:, :H].reshape(steps, requests, KV, group, HD)
    new_keys = rotated[:, H:].reshape(steps, requests, KV * HD)
    new_values = projected[:, (H + KV) * HD :].reshape(steps, requests, KV * HD)
    slot_keys = jnp.take(new_keys, owner, axis=1)
    slot_values = jnp.take(new_values, owner, axis=1)
    for step in range(steps):
        write_here = jnp.logical_and(live[:, None], positions == (slot_length + step)[:, None])[
            :, :, None
        ]
        key_cache = jnp.where(write_here, slot_keys[step][:, None, :], key_cache)
        value_cache = jnp.where(write_here, slot_values[step][:, None, :], value_cache)
    slot_queries = jnp.take(queries, owner, axis=1)
    keys_view = key_cache.reshape(slots, per_page, KV, HD)
    values_view = value_cache.reshape(slots, per_page, KV, HD)
    scores = (
        jnp.einsum("tjkgd,jpkd->jktgp", slot_queries, keys_view, preferred_element_type=jnp.float32)
        * scale
    )
    last = slot_length[:, None] + jnp.arange(steps, dtype=jnp.int32)[None, :]
    valid = jnp.logical_and(live[:, None, None], positions[:, None, :] <= last[:, :, None])[
        :, None, :, None, :
    ]
    masked = jnp.where(valid, scores, NEGATIVE)
    page_max = jnp.max(masked, axis=4)
    weights = jnp.where(valid, jnp.exp(masked - page_max[..., None]), 0.0).astype(jnp.bfloat16)
    page_sum = jnp.sum(weights.astype(jnp.float32), axis=4)
    page_acc = jnp.einsum(
        "jktgp,jpkd->jktgd", weights, values_view, preferred_element_type=jnp.float32
    )
    spread = owned[:, :, None, None, None]
    candidates = jnp.where(spread, page_max[:, None], NEGATIVE)
    top = jnp.max(candidates, axis=0)
    factor = jnp.where(spread, jnp.exp(candidates - top[None]), 0.0)
    total = jnp.sum(factor * page_sum[:, None], axis=0)
    summed = jnp.sum(factor[..., None] * page_acc[:, None], axis=0)

    def by_head(value):
        value = jnp.moveaxis(value, 0, 3)
        value = jnp.swapaxes(value, 1, 2)
        return value.reshape((seq, H // seq, rows) + value.shape[4:])

    packed = jnp.concatenate(
        [
            by_head(summed).reshape(seq, -1),
            by_head(top).reshape(seq, -1),
            by_head(total).reshape(seq, -1),
        ],
        axis=1,
    )
    packed = lax.all_to_all(packed, "seq", split_axis=0, concat_axis=0, tiled=True)
    count = H // seq * rows
    part_acc = packed[:, : count * HD].reshape(seq, count, HD)
    part_top = packed[:, count * HD : count * (HD + 1)]
    part_sum = packed[:, count * (HD + 1) :]
    best = jnp.max(part_top, axis=0)
    share = jnp.exp(part_top - best[None])
    denominator = jnp.sum(share * part_sum, axis=0)
    numerator = jnp.sum(share[..., None] * part_acc, axis=0)
    heads = (numerator / denominator[:, None]).astype(jnp.bfloat16)
    heads = jnp.swapaxes(heads.reshape(H // seq, rows, HD), 0, 1).reshape(rows, -1)
    attended = lax.all_gather(heads, "seq", axis=1, tiled=True)
    branch_out = jnp.dot(
        attended, w_out.reshape(H * HD, blocks * pieces), preferred_element_type=jnp.float32
    ).reshape(rows, blocks, pieces)
    current = hidden_in.reshape(rows, blocks, pieces).astype(jnp.float32)
    middle = (current + branch_out).astype(jnp.bfloat16)
    rows_mid = lax.all_gather(middle, "seq", axis=2, tiled=True).astype(jnp.float32)
    inverse = lax.rsqrt(jnp.mean(rows_mid * rows_mid, axis=(1, 2), keepdims=True) + EPSILON)
    normed_mid = (rows_mid * inverse * norm_mlp.reshape(blocks, quarter)).astype(jnp.bfloat16)
    mine = lax.all_to_all(normed_mid, "req", split_axis=1, concat_axis=0, tiled=True).reshape(
        -1, quarter
    )
    gate_part = jnp.dot(mine, w_gate, preferred_element_type=jnp.float32).astype(jnp.bfloat16)
    up_part = jnp.dot(mine, w_up, preferred_element_type=jnp.float32).astype(jnp.bfloat16)
    gate_sum = lax.psum_scatter(gate_part, "req", scatter_dimension=0, tiled=True)
    up_sum = lax.psum_scatter(up_part, "req", scatter_dimension=0, tiled=True)
    hidden_part = (jax.nn.silu(gate_sum.astype(jnp.float32)) * up_sum.astype(jnp.float32)).astype(
        jnp.bfloat16
    )
    hidden = lax.all_gather(hidden_part, "req", axis=0, tiled=True)
    down = jnp.dot(hidden, w_down, preferred_element_type=jnp.float32)
    sums = lax.psum_scatter(
        down.reshape(down.shape[0], 1, quarter).astype(jnp.bfloat16),
        "seq",
        scatter_dimension=2,
        tiled=True,
    ).astype(jnp.float32)
    back = lax.all_to_all(sums, "req", split_axis=0, concat_axis=1, tiled=True)
    output = (middle.astype(jnp.float32) + back).astype(jnp.bfloat16)
    return (output.reshape(hidden_in.shape), key_cache, value_cache)


def solution(mesh):
    in_specs = (
        P(None, "req", None, "seq"),
        P("req"),
        P("req", None),
        P(("req", "seq"), None, None),
        P(("req", "seq"), None, None),
        P(),
        P(None, "seq"),
        P("seq"),
        P(None, None, "seq"),
        P(),
        P("req", "seq"),
        P("req", "seq"),
        P("seq", "req"),
    )
    out_specs = (
        P(None, "req", None, "seq"),
        P(("req", "seq"), None, None),
        P(("req", "seq"), None, None),
    )
    return jax.shard_map(
        on_device, mesh=mesh, in_specs=in_specs, out_specs=out_specs, check_vma=False
    )
```

profile of v0, /device:TPU:0, one launch (start us, length us, event | category | flops | bytes accessed | tf_op | source)
XLA Modules:
  0.0 303.2 jit_solution(10138137191504181131)
XLA Ops:
  7.2 1.0 compare_reduce_fusion
  8.2 1.1 fusion.33
  9.3 11.7 %all_gather.15 = bf16[4,8,4,2048]{3,2,1,0:T(4,128)(2,1)S(1)} all-gather(bf16[4,8,4,256]{3,2,1,0:T(4,128)(2,1)} %param.15), channel_id=1, replica_groups=mesh['req'=4,'seq'=8] {'seq'}, dimensions={3}, use_global_device_ids=true | all-gather | bytes 589824 | tf_op jit(solution)/shard_map/all_gather | solution.py:67
  22.2 9.0 %fusion.1 = bf16[32,1280]{1,0:T(8,128)(2,1)S(1)} fusion(bf16[8192,1280]{1,0:T(8,128)(2,1)} %param.21, f32[32,8192]{1,0:T(8,128)S(1)} %bitcast.124, f32[8192]{0:T(1024)S(1)} %copy-done.5, f32[32]{0:T(128)S(1)} %rsqrt.20, f32[1280]{0:T(1024)S(1)} %convert_element_type.96), kind=kOutput, calls=%fused_computation.9 | convolution fusion | flops 671956992 | bytes 22140032 | tf_op jit(solution)/shard_map/dot_general | solution.py:72
  31.2 10.3 %all_gather.16 = bf16[32,10240]{1,0:T(8,128)(2,1)S(1)} all-gather(bf16[32,1280]{1,0:T(8,128)(2,1)S(1)} %fusion.1), channel_id=1, replica_groups=mesh['req'=4,'seq'=8] {'seq'}, dimensions={1}, use_global_device_ids=true | all-gather | bytes 737280 | tf_op jit(solution)/shard_map/all_gather | solution.py:74
  45.7 2.8 select_select_fusion
  49.0 0.7 copy-done.1
  49.7 1.4 bitcast_bitcast_fusion.1
  51.8 2.7 fusion.48
  54.6 0.7 convert_reduce_fusion
  57.1 1.0 copy-done.3
  58.2 0.7 fusion.2
  59.1 2.3 multiply_reduce_fusion
  62.7 2.1 copy.101
  64.8 3.6 %all-to-all-start = ((f32[8,1,33280]{2,1,0:T(1,128)}), f32[8,1,33280]{2,1,0:T(1,128)S(1)}, u32[]{:S(2)}, u32[]{:S(2)}) async-start(f32[8,1,33280]{2,1,0:T(1,128)} %copy.101), calls=%async_computation | async-start | bytes 2129920 | tf_op jit(solution)/shard_map/all_to_all | solution.py:128
  68.6 16.8 %copy.129 = bf16[1024,8,4,256]{3,1,2,0:T(8,128)(2,1)} copy(bf16[1024,8,4,256]{3,2,1,0:T(4,128)(2,1)} %bitcast.118) | data formatting | bytes 33554432
  85.4 20.9 %copy.104 = bf16[1024,8192]{1,0:T(8,128)(2,1)} copy(bf16[1024,8192]{0,1:T(8,128)(2,1)} %bitcast.117) | data formatting | bytes 33554432 | tf_op jit(solution)/shard_map/dot_general | solution.py:140
  107.2 10.0 %all_gather.17 = bf16[32,8192]{1,0:T(8,128)(2,1)S(1)} all-gather(bf16[32,1024]{1,0:T(8,128)(2,1)S(1)} %copy_bitcast_fusion.2), channel_id=1, replica_groups=mesh['req'=4,'seq'=8] {'seq'}, dimensions={1}, use_global_device_ids=true | all-gather | bytes 589824 | tf_op jit(solution)/shard_map/all_gather | solution.py:139
  117.2 10.8 %fusion.12 = bf16[32,4,256]{2,0,1:T(8,128)(2,1)S(1)} fusion(bf16[4,256,8192]{2,1,0:T(8,128)(2,1)} %bitcast.116, bf16[32,8192]{1,0:T(8,128)(2,1)S(1)} %all_gather.17, f32[4,8,4,256]{3,2,1,0:T(4,128)S(1)} %convert_element_type.118), kind=kOutput, calls=%fused_computation.30 | convolution fusion | flops 536936448 | bytes 17498112 | tf_op jit(solution)/shard_map/dot_general | solution.py:140
  128.0 11.2 %all_gather.18 = bf16[32,4,2048]{2,0,1:T(8,128)(2,1)S(1)} all-gather(bf16[32,4,256]{2,0,1:T(8,128)(2,1)S(1)} %fusion.12), channel_id=1, replica_groups=mesh['req'=4,'seq'=8] {'seq'}, dimensions={2}, use_global_device_ids=true | all-gather | bytes 589824 | tf_op jit(solution)/shard_map/all_gather | solution.py:145
  139.7 19.7 %all_to_all.45 = bf16[32,4,2048]{2,0,1:T(8,128)(2,1)S(1)} all-to-all(bf16[32,4,2048]{2,0,1:T(8,128)(2,1)S(1)} %fusion.15), channel_id=1, replica_groups=mesh['req'=4,'seq'=8] {'req'}, dimensions={1} | all-to-all | bytes 1048576 | tf_op jit(solution)/shard_map/all_to_all | solution.py:148
  159.4 11.3 %convolution_convert_fusion = bf16[128,3696]{1,0:T(8,128)(2,1)} fusion(bf16[128,2048]{1,0:T(8,128)(2,1)S(1)} %bitcast.125, bf16[2048,3696]{0,1:T(8,128)(2,1)} %param.26), kind=kOutput, calls=%fused_computation.4 | convolution fusion | flops 1938241536 | bytes 16609280 | tf_op jit(solution)/shard_map/dot_general | solution.py:152
  171.0 11.5 %convolution_convert_fusion.1 = bf16[128,3696]{1,0:T(8,128)(2,1)} fusion(bf16[128,2048]{1,0:T(8,128)(2,1)S(1)} %bitcast.126, bf16[2048,3696]{0,1:T(8,128)(2,1)} %param.25), kind=kOutput, calls=%fused_computation.5 | convolution fusion | flops 1938241536 | bytes 16609280 | tf_op jit(solution)/shard_map/dot_general | solution.py:151
  182.6 12.0 %reduce-scatter.6.cloned.1.call-done = bf16[32,3696]{1,0:T(8,128)(2,1)} async-done(((bf16[128,3696]{1,0:T(8,128)(2,1)}), bf16[32,3696]{1,0:T(8,128)(2,1)}) %reduce-scatter.6.cloned.1.call-update) | async-done | bytes 236560 | tf_op jit(solution)/shard_map/reduce_scatter | solution.py:154
  194.6 26.8 %reduce-scatter.4.cloned.1.call-done = bf16[32,3696]{1,0:T(8,128)(2,1)} async-done(((bf16[128,3696]{1,0:T(8,128)(2,1)}), bf16[32,3696]{1,0:T(8,128)(2,1)}) %reduce-scatter.4.cloned.1.call-update) | async-done | bytes 236560 | tf_op jit(solution)/shard_map/reduce_scatter | solution.py:153
  221.4 1.2 fusion.28
  222.6 19.6 %all_gather.19 = bf16[128,3696]{1,0:T(8,128)(2,1)S(1)} all-gather(bf16[32,3696]{1,0:T(8,128)(2,1)S(1)} %fusion.28), channel_id=1, replica_groups=mesh['req'=4,'seq'=8] {'req'}, dimensions={0}, use_global_device_ids=true | all-gather | bytes 1182720 | tf_op jit(solution)/shard_map/all_gather | solution.py:158
  242.3 8.5 %fusion = bf16[128,1,2048]{2,0,1:T(8,128)(2,1)} fusion(bf16[128,3696]{1,0:T(8,128)(2,1)S(1)} %all_gather.19, bf16[3696,2048]{1,0:T(8,128)(2,1)} %param.27), kind=kOutput, calls=%fused_computation.7 | convolution fusion | flops 1938030592 | bytes 16609280 | tf_op jit(solution)/shard_map/dot_general | solution.py:159
  250.8 33.8 %reduce-scatter.8.cloned.1.call-done = bf16[128,1,256]{2,0,1:T(8,128)(2,1)} async-done(((bf16[128,1,2048]{2,0,1:T(8,128)(2,1)}), bf16[128,1,256]{2,0,1:T(8,128)(2,1)}) %reduce-scatter.8.cloned.1.call-update) | async-done | bytes 65552 | tf_op jit(solution)/shard_map/reduce_scatter | solution.py:160
  284.6 0.9 copy.105
  285.6 10.3 %all_to_all.46 = f32[128,1,256]{2,1,0:T(1,128)S(1)} all-to-all(f32[128,1,256]{2,1,0:T(1,128)S(1)} %copy.105), channel_id=1, replica_groups=mesh['req'=4,'seq'=8] {'req'}, dimensions={0} | all-to-all | bytes 262144 | tf_op jit(solution)/shard_map/all_to_all | solution.py:166
  295.9 0.7 copy.106
  (97 shorter events, 11.8 us)
Async XLA Ops:
  21.0 1.2 copy-start.7
  21.0 1.2 copy-start.5
  41.5 0.7 copy-start.8
  48.5 1.2 copy-start.1
  48.5 7.9 %copy-start = (bf16[7,128,1024]{2,1,0:T(8,128)(2,1)}, bf16[7,128,1024]{2,1,0:T(8,128)(2,1)S(1)}, u32[]{:S(2)}) copy-start(bf16[7,128,1024]{2,1,0:T(8,128)(2,1)S(1)} %get-tuple-element.41) | copy-start | bytes 5505028
  54.5 1.2 copy-start.2
  57.0 1.2 copy-start.3
  62.7 5.9 %copy-start.4 = (bf16[4,8,4,256]{3,2,1,0:T(4,128)(2,1)S(1)}, bf16[4,8,4,256]{3,2,1,0:T(4,128)(2,1)}, u32[]{:S(2)}) copy-start(bf16[4,8,4,256]{3,2,1,0:T(4,128)(2,1)} %param.15) | copy-start | bytes 196612
  64.8 41.6 %all-to-all-start = ((f32[8,1,33280]{2,1,0:T(1,128)}), f32[8,1,33280]{2,1,0:T(1,128)S(1)}, u32[]{:S(2)}, u32[]{:S(2)}) async-start(f32[8,1,33280]{2,1,0:T(1,128)} %copy.101), calls=%async_computation | async-start | bytes 2129920 | tf_op jit(solution)/shard_map/all_to_all | solution.py:128
  68.3 126.3 %reduce-scatter.6.cloned.1.call-start = ((), (), s32[]{:S(2)}) async-start(), calls=%async_computation.7 | async-start | bytes 1187840 | tf_op jit(solution)/shard_map/reduce_scatter | solution.py:154
  85.4 20.9 %copy-start.6 = (f32[8192]{0:T(1024)S(1)}, f32[8192]{0:T(1024)}, u32[]{:S(2)}) copy-start(f32[8192]{0:T(1024)} %param.24) | copy-start | bytes 98308
  170.7 50.7 %reduce-scatter.4.cloned.1.call-start = ((), (), s32[]{:S(2)}) async-start(), calls=%async_computation.6 | async-start | bytes 1187840 | tf_op jit(solution)/shard_map/reduce_scatter | solution.py:153
  182.5 102.1 %reduce-scatter.8.cloned.1.call-start = ((), (), s32[]{:S(2)}) async-start(), calls=%async_computation.8 | async-start | bytes 589824 | tf_op jit(solution)/shard_map/reduce_scatter | solution.py:160
Sparse Core Ops, SparseCore 0:
  170.8 23.7 reduce-scatter.5
  197.0 24.3 reduce-scatter.3
  250.9 33.6 reduce-scatter.7
where the time goes:
time: 305 us; the launch traced here: 303 us
  blocking collectives  92.9 us (30%)
  waiting for transfers between devices  72.7 us (24%)
  matrix products  54.4 us (18%)
  local copies, waits for them, and re-layouts  51.7 us (17%)
  between operations  14.2 us (5%)
  other arithmetic  13 us (4%)
  starting transfers between devices  4.16 us (1%)
    reduce_scatter x1, waiting for transfers between devices, on_device(): lax.psum_scatter(down.reshape(down.shape[0], 1, quarter).astype(jnp.bfloa...  33.8 us
    reduce_scatter x1, waiting for transfers between devices, on_device(): lax.psum_scatter(gate_part, 'req', scatter_dimension=0, tiled=True)  26.8 us
    unnamed x35, local copies, waits for them, and re-layouts  22.2 us
    dot_general x1, local copies, waits for them, and re-layouts, on_device(): jnp.dot(attended, w_out.reshape(H * HD, blocks * pieces), preferred_eleme...  20.9 us
    all_to_all x1, blocking collectives, on_device(): lax.all_to_all(normed_mid, 'req', split_axis=1, concat_axis=0, tiled=True)  19.7 us
    all_gather x1, blocking collectives, on_device(): hidden = lax.all_gather(hidden_part, 'req', axis=0, tiled=True)  19.6 us
    reduce_scatter x1, waiting for transfers between devices, on_device(): up_sum = lax.psum_scatter(up_part, 'req', scatter_dimension=0, tiled=True)  12 us
    all_gather x1, blocking collectives, on_device(): lax.all_gather(hidden_in, 'seq', axis=3, tiled=True).reshape(rows, D)  11.7 us
  transfers between devices with their start and end apart: 4, of which 3 were waited for; matrix products, arithmetic and copies ran while one was open for 16% of the time, Pallas kernels for 0%

commit v1 on v0

--- a/solution.py
+++ b/solution.py
@@ -1,3 +1,4 @@
+import functools
 import math
 import jax
 import jax.numpy as jnp
@@ -12,6 +13,25 @@
 EPSILON = 1e-06
 THETA = 1000000.0
 NEGATIVE = -1e30
+
+
+def begin_point_up(mat, device_axis):
+    n_slots = lax.psum(1, axis_name=device_axis)
+    grid = [mat]
+    num = 0
+    while num < n_slots - 1:
+        current_arr = lax.ppermute(
+            grid[-1], device_axis, [(dev_i, (dev_i + 1) % n_slots) for dev_i in range(n_slots)]
+        )
+        grid.append(current_arr)
+        num += 1
+    local_part = jnp.concatenate(grid[::-1], axis=1)
+    base_arr = lax.axis_index(device_axis)
+    r2 = jnp.roll(local_part, shift=(base_arr + 1) * mat.shape[1], axis=1)
+    return r2
+
+
+answer_spot = functools.partial(begin_point_up, device_axis="seq")
 
 
 def rotate(heads, position):
@@ -71,7 +91,7 @@
     columns = (
         jnp.dot(normed, w_qkv, preferred_element_type=jnp.float32) + b_qkv.astype(jnp.float32)
     ).astype(jnp.bfloat16)
-    projected = lax.all_gather(columns, "seq", axis=1, tiled=True)
+    projected = answer_spot(columns)
     position = (jnp.arange(steps, dtype=jnp.int32)[:, None] + cache_lens[None, :]).reshape(rows)
     rotated = rotate(
         projected[:, : (H + KV) * HD].reshape(rows, H + KV, HD).astype(jnp.float32), position

time: 305 us -> 325 us (1.066)
  waiting for transfers between devices: 72.7 us -> 104 us
  blocking collectives: 92.9 us -> 82.6 us
    ppermute x0 -> x7, waiting for transfers between devices: none -> 31.4 us  [begin_point_up(): lax.ppermute(grid[-1], device_axis, [(dev_i, (dev_i + 1) % n_slots) for d...]
    all_gather x1 -> x0, blocking collectives: 10.3 us -> none  [on_device(): projected = lax.all_gather(columns, 'seq', axis=1, tiled=True)]
    unnamed x35 -> x52, local copies, waits for them, and re-layouts: 22.2 us -> 22 us
  transfers between devices with their start and end apart: 4 -> 11, of which waited for: 3 -> 10; matrix products, arithmetic and copies ran while one was open for 16% -> 16% of each run, Pallas kernels for 0% -> 0%
where the time goes in v1:
time: 325 us; the launch traced here: 324 us
  waiting for transfers between devices  104 us (32%)
  blocking collectives  82.6 us (25%)
  matrix products  54.4 us (17%)
  local copies, waits for them, and re-layouts  51.6 us (16%)
  between operations  14.4 us (4%)
  other arithmetic  11.8 us (4%)
  starting transfers between devices  4.73 us (1%)
    reduce_scatter x1, waiting for transfers between devices, on_device(): lax.psum_scatter(down.reshape(down.shape[0], 1, quarter).astype(jnp.bfloa...  33.9 us
    ppermute x7, waiting for transfers between devices, begin_point_up(): lax.ppermute(grid[-1], device_axis, [(dev_i, (dev_i + 1) % n_slots) for d...  31.4 us
    reduce_scatter x1, waiting for transfers between devices, on_device(): lax.psum_scatter(gate_part, 'req', scatter_dimension=0, tiled=True)  26.8 us
    unnamed x52, local copies, waits for them, and re-layouts  22 us
    dot_general x1, local copies, waits for them, and re-layouts, on_device(): jnp.dot(attended, w_out.reshape(H * HD, blocks * pieces), preferred_eleme...  20.9 us
    all_to_all x1, blocking collectives, on_device(): lax.all_to_all(normed_mid, 'req', split_axis=1, concat_axis=0, tiled=True)  19.7 us
    all_gather x1, blocking collectives, on_device(): hidden = lax.all_gather(hidden_part, 'req', axis=0, tiled=True)  19.7 us
    reduce_scatter x1, waiting for transfers between devices, on_device(): up_sum = lax.psum_scatter(up_part, 'req', scatter_dimension=0, tiled=True)  12 us
  transfers between devices with their start and end apart: 11, of which 10 were waited for; matrix products, arithmetic and copies ran while one was open for 16% of the time, Pallas kernels for 0%

profile of v1, /device:TPU:0, one launch (start us, length us, event | category | flops | bytes accessed | tf_op | source)
XLA Modules:
  0.0 323.7 jit_solution(18245377537429550827)
XLA Ops:
  7.2 11.7 %all_gather.12 = bf16[4,8,4,2048]{3,2,1,0:T(4,128)(2,1)S(1)} all-gather(bf16[4,8,4,256]{3,2,1,0:T(4,128)(2,1)} %param.15), channel_id=1, replica_groups=mesh['req'=4,'seq'=8] {'seq'}, dimensions={3}, use_global_device_ids=true | all-gather | bytes 589824 | tf_op jit(solution)/shard_map/all_gather | solution.py:87
  20.2 9.0 %fusion.1 = bf16[32,1280]{1,0:T(8,128)(2,1)S(1)} fusion(bf16[8192,1280]{1,0:T(8,128)(2,1)} %param.21, f32[32,8192]{1,0:T(8,128)S(1)} %bitcast.124, f32[8192]{0:T(1024)S(1)} %copy-done.5, f32[32]{0:T(128)S(1)} %rsqrt.20, f32[1280]{0:T(1024)S(1)} %convert_element_type.96), kind=kOutput, calls=%fused_computation.9 | convolution fusion | flops 671956992 | bytes 22140032 | tf_op jit(solution)/shard_map/dot_general | solution.py:92
  31.0 3.0 collective-permute-done
  34.0 4.7 %collective-permute-done.1 = bf16[32,1280]{1,0:T(8,128)(2,1)S(1)} collective-permute-done((bf16[32,1280]{1,0:T(8,128)(2,1)S(1)}, bf16[32,1280]{1,0:T(8,128)(2,1)S(1)}, u32[]{:S(2)}, u32[]{:S(2)}) %collective-permute-start.1) | collective-permute-done | bytes 81952 | tf_op jit(solution)/shard_map/ppermute | solution.py:23
  38.8 4.7 %collective-permute-done.2 = bf16[32,1280]{1,0:T(8,128)(2,1)S(1)} collective-permute-done((bf16[32,1280]{1,0:T(8,128)(2,1)S(1)}, bf16[32,1280]{1,0:T(8,128)(2,1)S(1)}, u32[]{:S(2)}, u32[]{:S(2)}) %collective-permute-start.2) | collective-permute-done | bytes 81952 | tf_op jit(solution)/shard_map/ppermute | solution.py:23
  43.5 4.8 %collective-permute-done.3 = bf16[32,1280]{1,0:T(8,128)(2,1)S(1)} collective-permute-done((bf16[32,1280]{1,0:T(8,128)(2,1)S(1)}, bf16[32,1280]{1,0:T(8,128)(2,1)S(1)}, u32[]{:S(2)}, u32[]{:S(2)}) %collective-permute-start.3) | collective-permute-done | bytes 81952 | tf_op jit(solution)/shard_map/ppermute | solution.py:23
  48.3 4.8 %collective-permute-done.4 = bf16[32,1280]{1,0:T(8,128)(2,1)S(1)} collective-permute-done((bf16[32,1280]{1,0:T(8,128)(2,1)S(1)}, bf16[32,1280]{1,0:T(8,128)(2,1)S(1)}, u32[]{:S(2)}, u32[]{:S(2)}) %collective-permute-start.4) | collective-permute-done | bytes 81952 | tf_op jit(solution)/shard_map/ppermute | solution.py:23
  53.0 4.8 %collective-permute-done.5 = bf16[32,1280]{1,0:T(8,128)(2,1)S(1)} collective-permute-done((bf16[32,1280]{1,0:T(8,128)(2,1)S(1)}, bf16[32,1280]{1,0:T(8,128)(2,1)S(1)}, u32[]{:S(2)}, u32[]{:S(2)}) %collective-permute-start.5) | collective-permute-done | bytes 81952 | tf_op jit(solution)/shard_map/ppermute | solution.py:23
  57.8 4.8 %collective-permute-done.6 = bf16[32,1280]{1,0:T(8,128)(2,1)S(1)} collective-permute-done((bf16[32,1280]{1,0:T(8,128)(2,1)S(1)}, bf16[32,1280]{1,0:T(8,128)(2,1)S(1)}, u32[]{:S(2)}, u32[]{:S(2)}) %collective-permute-start.6) | collective-permute-done | bytes 81952 | tf_op jit(solution)/shard_map/ppermute | solution.py:23
  66.1 2.8 select_select_fusion
  70.2 1.4 bitcast_bitcast_fusion.1
  72.2 2.7 fusion.48
  77.5 1.0 copy-done.3
  79.5 2.3 multiply_reduce_fusion
  83.1 2.1 copy.101
  85.2 3.7 %all-to-all-start = ((f32[8,1,33280]{2,1,0:T(1,128)}), f32[8,1,33280]{2,1,0:T(1,128)S(1)}, u32[]{:S(2)}, u32[]{:S(2)}) async-start(f32[8,1,33280]{2,1,0:T(1,128)} %copy.101), calls=%async_computation | async-start | bytes 2129920 | tf_op jit(solution)/shard_map/all_to_all | solution.py:148
  89.2 16.8 %copy.129 = bf16[1024,8,4,256]{3,1,2,0:T(8,128)(2,1)} copy(bf16[1024,8,4,256]{3,2,1,0:T(4,128)(2,1)} %bitcast.118) | data formatting | bytes 33554432
  105.9 20.9 %copy.104 = bf16[1024,8192]{1,0:T(8,128)(2,1)} copy(bf16[1024,8192]{0,1:T(8,128)(2,1)} %bitcast.117) | data formatting | bytes 33554432 | tf_op jit(solution)/shard_map/dot_general | solution.py:160
  127.7 10.0 %all_gather.13 = bf16[32,8192]{1,0:T(8,128)(2,1)S(1)} all-gather(bf16[32,1024]{1,0:T(8,128)(2,1)S(1)} %copy_bitcast_fusion.2), channel_id=1, replica_groups=mesh['req'=4,'seq'=8] {'seq'}, dimensions={1}, use_global_device_ids=true | all-gather | bytes 589824 | tf_op jit(solution)/shard_map/all_gather | solution.py:159
  137.7 10.8 %fusion.12 = bf16[32,4,256]{2,0,1:T(8,128)(2,1)S(1)} fusion(bf16[4,256,8192]{2,1,0:T(8,128)(2,1)} %bitcast.116, bf16[32,8192]{1,0:T(8,128)(2,1)S(1)} %all_gather.13, f32[4,8,4,256]{3,2,1,0:T(4,128)S(1)} %convert_element_type.118), kind=kOutput, calls=%fused_computation.30 | convolution fusion | flops 536936448 | bytes 17498112 | tf_op jit(solution)/shard_map/dot_general | solution.py:160
  148.6 11.2 %all_gather.14 = bf16[32,4,2048]{2,0,1:T(8,128)(2,1)S(1)} all-gather(bf16[32,4,256]{2,0,1:T(8,128)(2,1)S(1)} %fusion.12), channel_id=1, replica_groups=mesh['req'=4,'seq'=8] {'seq'}, dimensions={2}, use_global_device_ids=true | all-gather | bytes 589824 | tf_op jit(solution)/shard_map/all_gather | solution.py:165
  160.2 19.7 %all_to_all.45 = bf16[32,4,2048]{2,0,1:T(8,128)(2,1)S(1)} all-to-all(bf16[32,4,2048]{2,0,1:T(8,128)(2,1)S(1)} %fusion.15), channel_id=1, replica_groups=mesh['req'=4,'seq'=8] {'req'}, dimensions={1} | all-to-all | bytes 1048576 | tf_op jit(solution)/shard_map/all_to_all | solution.py:168
  179.9 11.3 %convolution_convert_fusion = bf16[128,3696]{1,0:T(8,128)(2,1)} fusion(bf16[128,2048]{1,0:T(8,128)(2,1)S(1)} %bitcast.125, bf16[2048,3696]{0,1:T(8,128)(2,1)} %param.26), kind=kOutput, calls=%fused_computation.4 | convolution fusion | flops 1938241536 | bytes 16609280 | tf_op jit(solution)/shard_map/dot_general | solution.py:172
  191.5 11.5 %convolution_convert_fusion.1 = bf16[128,3696]{1,0:T(8,128)(2,1)} fusion(bf16[128,2048]{1,0:T(8,128)(2,1)S(1)} %bitcast.126, bf16[2048,3696]{0,1:T(8,128)(2,1)} %param.25), kind=kOutput, calls=%fused_computation.5 | convolution fusion | flops 1938241536 | bytes 16609280 | tf_op jit(solution)/shard_map/dot_general | solution.py:171
  203.1 12.0 %reduce-scatter.6.cloned.1.call-done = bf16[32,3696]{1,0:T(8,128)(2,1)} async-done(((bf16[128,3696]{1,0:T(8,128)(2,1)}), bf16[32,3696]{1,0:T(8,128)(2,1)}) %reduce-scatter.6.cloned.1.call-update) | async-done | bytes 236560 | tf_op jit(solution)/shard_map/reduce_scatter | solution.py:174
  215.1 26.8 %reduce-scatter.4.cloned.1.call-done = bf16[32,3696]{1,0:T(8,128)(2,1)} async-done(((bf16[128,3696]{1,0:T(8,128)(2,1)}), bf16[32,3696]{1,0:T(8,128)(2,1)}) %reduce-scatter.4.cloned.1.call-update) | async-done | bytes 236560 | tf_op jit(solution)/shard_map/reduce_scatter | solution.py:173
  241.9 1.2 fusion.28
  243.1 19.7 %all_gather.15 = bf16[128,3696]{1,0:T(8,128)(2,1)S(1)} all-gather(bf16[32,3696]{1,0:T(8,128)(2,1)S(1)} %fusion.28), channel_id=1, replica_groups=mesh['req'=4,'seq'=8] {'req'}, dimensions={0}, use_global_device_ids=true | all-gather | bytes 1182720 | tf_op jit(solution)/shard_map/all_gather | solution.py:178
  262.8 8.5 %fusion = bf16[128,1,2048]{2,0,1:T(8,128)(2,1)} fusion(bf16[128,3696]{1,0:T(8,128)(2,1)S(1)} %all_gather.15, bf16[3696,2048]{1,0:T(8,128)(2,1)} %param.27), kind=kOutput, calls=%fused_computation.7 | convolution fusion | flops 1938030592 | bytes 16609280 | tf_op jit(solution)/shard_map/dot_general | solution.py:179
  271.3 33.9 %reduce-scatter.8.cloned.1.call-done = bf16[128,1,256]{2,0,1:T(8,128)(2,1)} async-done(((bf16[128,1,2048]{2,0,1:T(8,128)(2,1)}), bf16[128,1,256]{2,0,1:T(8,128)(2,1)}) %reduce-scatter.8.cloned.1.call-update) | async-done | bytes 65552 | tf_op jit(solution)/shard_map/reduce_scatter | solution.py:180
  305.2 0.9 copy.105
  306.1 10.3 %all_to_all.46 = f32[128,1,256]{2,1,0:T(1,128)S(1)} all-to-all(f32[128,1,256]{2,1,0:T(1,128)S(1)} %copy.105), channel_id=1, replica_groups=mesh['req'=4,'seq'=8] {'req'}, dimensions={0} | all-to-all | bytes 262144 | tf_op jit(solution)/shard_map/all_to_all | solution.py:186
  (129 shorter events, 15.7 us)
Async XLA Ops:
  19.0 1.1 copy-start.8
  19.0 1.1 copy-start.5
  20.1 9.4 %copy-start.7 = (s32[8,32]{1,0:T(8,128)S(1)}, s32[8,32]{1,0:T(8,128)}, u32[]{:S(2)}) copy-start(s32[8,32]{1,0:T(8,128)} %param.17) | copy-start | bytes 3076
  20.2 10.1 %copy-start.9 = (s32[8]{0:T(128)S(1)}, s32[8]{0:T(128)}, u32[]{:S(2)}) copy-start(s32[8]{0:T(128)} %param.16) | copy-start | bytes 100
  29.1 4.8 %collective-permute-start = (bf16[32,1280]{1,0:T(8,128)(2,1)S(1)}, bf16[32,1280]{1,0:T(8,128)(2,1)S(1)}, u32[]{:S(2)}, u32[]{:S(2)}) collective-permute-start(bf16[32,1280]{1,0:T(8,128)(2,1)S(1)} %fusion.1), channel_id=1, source_target_pairs={{0,1},{1,2},{2,3},{3,4},{4,5},{5,6},{6,7},{7,0},{8,9},{9,10},{10,1... | collective-permute-start | bytes 245768 | tf_op jit(solution)/shard_map/ppermute | solution.py:23
  34.0 4.8 %collective-permute-start.1 = (bf16[32,1280]{1,0:T(8,128)(2,1)S(1)}, bf16[32,1280]{1,0:T(8,128)(2,1)S(1)}, u32[]{:S(2)}, u32[]{:S(2)}) collective-permute-start(bf16[32,1280]{1,0:T(8,128)(2,1)S(1)} %collective-permute-done), channel_id=1, source_target_pairs={{0,1},{1,2},{2,3},{3,4},{4,5},{5,6},{6,7},{7,0},{8,9},{9,10},{10,1... | collective-permute-start | bytes 245768 | tf_op jit(solution)/shard_map/ppermute | solution.py:23
  38.7 4.8 %collective-permute-start.2 = (bf16[32,1280]{1,0:T(8,128)(2,1)S(1)}, bf16[32,1280]{1,0:T(8,128)(2,1)S(1)}, u32[]{:S(2)}, u32[]{:S(2)}) collective-permute-start(bf16[32,1280]{1,0:T(8,128)(2,1)S(1)} %collective-permute-done.1), channel_id=1, source_target_pairs={{0,1},{1,2},{2,3},{3,4},{4,5},{5,6},{6,7},{7,0},{8,9},{9,10},{10,1... | collective-permute-start | bytes 245768 | tf_op jit(solution)/shard_map/ppermute | solution.py:23
  43.5 4.8 %collective-permute-start.3 = (bf16[32,1280]{1,0:T(8,128)(2,1)S(1)}, bf16[32,1280]{1,0:T(8,128)(2,1)S(1)}, u32[]{:S(2)}, u32[]{:S(2)}) collective-permute-start(bf16[32,1280]{1,0:T(8,128)(2,1)S(1)} %collective-permute-done.2), channel_id=1, source_target_pairs={{0,1},{1,2},{2,3},{3,4},{4,5},{5,6},{6,7},{7,0},{8,9},{9,10},{10,1... | collective-permute-start | bytes 245768 | tf_op jit(solution)/shard_map/ppermute | solution.py:23
  48.2 4.8 %collective-permute-start.4 = (bf16[32,1280]{1,0:T(8,128)(2,1)S(1)}, bf16[32,1280]{1,0:T(8,128)(2,1)S(1)}, u32[]{:S(2)}, u32[]{:S(2)}) collective-permute-start(bf16[32,1280]{1,0:T(8,128)(2,1)S(1)} %collective-permute-done.3), channel_id=1, source_target_pairs={{0,1},{1,2},{2,3},{3,4},{4,5},{5,6},{6,7},{7,0},{8,9},{9,10},{10,1... | collective-permute-start | bytes 245768 | tf_op jit(solution)/shard_map/ppermute | solution.py:23
  53.0 4.8 %collective-permute-start.5 = (bf16[32,1280]{1,0:T(8,128)(2,1)S(1)}, bf16[32,1280]{1,0:T(8,128)(2,1)S(1)}, u32[]{:S(2)}, u32[]{:S(2)}) collective-permute-start(bf16[32,1280]{1,0:T(8,128)(2,1)S(1)} %collective-permute-done.4), channel_id=1, source_target_pairs={{0,1},{1,2},{2,3},{3,4},{4,5},{5,6},{6,7},{7,0},{8,9},{9,10},{10,1... | collective-permute-start | bytes 245768 | tf_op jit(solution)/shard_map/ppermute | solution.py:23
  57.8 4.8 %collective-permute-start.6 = (bf16[32,1280]{1,0:T(8,128)(2,1)S(1)}, bf16[32,1280]{1,0:T(8,128)(2,1)S(1)}, u32[]{:S(2)}, u32[]{:S(2)}) collective-permute-start(bf16[32,1280]{1,0:T(8,128)(2,1)S(1)} %collective-permute-done.5), channel_id=1, source_target_pairs={{0,1},{1,2},{2,3},{3,4},{4,5},{5,6},{6,7},{7,0},{8,9},{9,10},{10,1... | collective-permute-start | bytes 245768 | tf_op jit(solution)/shard_map/ppermute | solution.py:23
  69.0 1.2 copy-start.1
  69.0 7.8 %copy-start = (bf16[7,128,1024]{2,1,0:T(8,128)(2,1)}, bf16[7,128,1024]{2,1,0:T(8,128)(2,1)S(1)}, u32[]{:S(2)}) copy-start(bf16[7,128,1024]{2,1,0:T(8,128)(2,1)S(1)} %get-tuple-element.41) | copy-start | bytes 5505028
  74.9 1.2 copy-start.2
  77.4 1.2 copy-start.3
  85.2 4.0 %copy-start.4 = (bf16[4,8,4,256]{3,2,1,0:T(4,128)(2,1)S(1)}, bf16[4,8,4,256]{3,2,1,0:T(4,128)(2,1)}, u32[]{:S(2)}) copy-start(bf16[4,8,4,256]{3,2,1,0:T(4,128)(2,1)} %param.15) | copy-start | bytes 196612
  85.2 41.7 %all-to-all-start = ((f32[8,1,33280]{2,1,0:T(1,128)}), f32[8,1,33280]{2,1,0:T(1,128)S(1)}, u32[]{:S(2)}, u32[]{:S(2)}) async-start(f32[8,1,33280]{2,1,0:T(1,128)} %copy.101), calls=%async_computation | async-start | bytes 2129920 | tf_op jit(solution)/shard_map/all_to_all | solution.py:148
  88.9 126.3 %reduce-scatter.6.cloned.1.call-start = ((), (), s32[]{:S(2)}) async-start(), calls=%async_computation.7 | async-start | bytes 1187840 | tf_op jit(solution)/shard_map/reduce_scatter | solution.py:174
  105.9 20.9 %copy-start.6 = (f32[8192]{0:T(1024)S(1)}, f32[8192]{0:T(1024)}, u32[]{:S(2)}) copy-start(f32[8192]{0:T(1024)} %param.24) | copy-start | bytes 98308
  191.2 50.7 %reduce-scatter.4.cloned.1.call-start = ((), (), s32[]{:S(2)}) async-start(), calls=%async_computation.6 | async-start | bytes 1187840 | tf_op jit(solution)/shard_map/reduce_scatter | solution.py:173
  203.1 102.1 %reduce-scatter.8.cloned.1.call-start = ((), (), s32[]{:S(2)}) async-start(), calls=%async_computation.8 | async-start | bytes 589824 | tf_op jit(solution)/shard_map/reduce_scatter | solution.py:180
Sparse Core Ops, SparseCore 0:
  191.3 23.7 reduce-scatter.5
  217.5 24.3 reduce-scatter.3
  271.4 33.6 reduce-scatter.7
